TPU v7x, 32 devices: a whole 2x2x4 slice. The times are simulated.
32 devices in a mesh: clip: 2 (over x), frame: 8 (over z, y), band: 2 (over core).
Axes of the slice: x: 2, y: 2, z: 4, core: 2. Of those that a mesh axis runs over, the one named last changes fastest.
Arguments:
- pixels: bfloat16 [16, 16, 32, 256], P(('clip', 'frame'), 'band'), parts along dimension 0, may hold values from -40 to 40
- gru_state: bfloat16 [16, 16, 32, 128], P(('clip', 'frame'), 'band'), parts along dimension 0, may hold values from -1 to 1
- tokens: bfloat16 [16, 1024, 256], P(('clip', 'frame'), 'band'), parts along dimension 0, may hold values from -30 to 30
- visible: int32 [16, 1024], P(('clip', 'frame'), 'band'), parts along dimension 0, may hold values from 0 to 1, as said below
- query_frame: int32 [2048], P(('clip', 'band')), parts along dimension 0, may hold values from 0 to 7, as said below
- pixel_query: bfloat16 [256, 256], replicated, may hold values from -2 to 2
- pixel_key: bfloat16 [256, 256], replicated, may hold values from -2 to 2
- pixel_value: bfloat16 [256, 256], replicated, may hold values from -0.375 to 0.375
- pixel_out: bfloat16 [256, 128], replicated, may hold values from -1.5 to 1.5
- time_query: bfloat16 [256, 256], replicated, may hold values from -2 to 2
- time_key: bfloat16 [256, 256], replicated, may hold values from -2 to 2
- time_value: bfloat16 [256, 256], replicated, may hold values from -0.375 to 0.375
- time_out: bfloat16 [256, 256], replicated, may hold values from -0.75 to 0.75
- gru_gates: bfloat16 [3, 3, 256, 256], replicated, may hold values from -0.125 to 0.125
- gru_candidate: bfloat16 [3, 3, 256, 128], replicated, may hold values from -0.125 to 0.125
Outputs:
- refined_state: bfloat16 [16, 16, 32, 128], P(('clip', 'frame'), 'band'), parts along dimension 0
- track_out: bfloat16 [16, 1024, 256], P(('clip', 'frame'), 'band'), parts along dimension 0
There are 2 independent parts, one for each index of `clip`. A program takes and returns all parts, laid end to end along the dimension named above; an argument that names none is the same for every part. Nothing has to cross between parts.
Inputs may be any that keep to these rules, and one draw needn't show every extreme that they name: Each track is visible in the frame named by its query frame index. `query_frame`: every frame is the query frame of exactly 128 tracks.
All inputs are finite; a program needn't handle non-finite values.
Results may differ from a plain program's by a relative error of at most 0.0095.
The roundings to bfloat16 on the way count: a program that leaves them out, or rounds other values in their place, can miss the bound.
Values may be sent and summed in bfloat16 or wider, within the bound.
A program may use at most 64 MiB of HBM per device.

v0:
```python
import jax
import jax.numpy as jnp
from jax import lax
from jax.sharding import PartitionSpec as P

HEADS = 8
HEAD_DIM = 32
GRU_WIDTH = 128
ITERS = 2


def with_halo(x, sides, width):
    for axis, dim in sides:
        devices, length = (lax.axis_size(axis), x.shape[dim])
        up = [(i, (i + 1) % devices) for i in range(devices - 1)]
        down = [(j, i) for i, j in up]
        last = lax.slice_in_dim(x, length - width, length, axis=dim)
        first = lax.slice_in_dim(x, 0, width, axis=dim)
        before = lax.ppermute(last, axis, up)
        after = lax.ppermute(first, axis, down)
        x = jnp.concatenate([before, x, after], axis=dim)
    return x


def attend_heads(queries, key_rows, value_rows, key_mask):
    score_scale = HEAD_DIM ** (-0.5)
    head_outputs = []
    for head_index in range(HEADS):
        offset = head_index * HEAD_DIM
        scores = (
            jnp.dot(
                queries[:, offset : offset + HEAD_DIM],
                key_rows[:, offset : offset + HEAD_DIM].T,
                preferred_element_type=jnp.float32,
            )
            * score_scale
        )
        scores = jnp.where(key_mask[None, :], scores, -jnp.inf)
        weights = jax.nn.softmax(scores, axis=-1).astype(jnp.bfloat16)
        head_outputs.append(
            jnp.dot(
                weights,
                value_rows[:, offset : offset + HEAD_DIM],
                preferred_element_type=jnp.float32,
            )
        )
    return jnp.concatenate(head_outputs, axis=-1).astype(jnp.bfloat16)


def conv_rows(padded, weight, rows, columns):
    widened = jnp.pad(padded, ((0, 0), (1, 1), (0, 0)))
    summed = jnp.zeros((rows * columns, weight.shape[3]), jnp.float32)
    for row_shift in range(3):
        for col_shift in range(3):
            window = widened[row_shift : row_shift + rows, col_shift : col_shift + columns]
            summed = summed + jnp.dot(
                window.reshape(rows * columns, -1),
                weight[row_shift, col_shift],
                preferred_element_type=jnp.float32,
            )
    return summed


def temporal_core(query_part, key_part, value_part, seen_part, anchor_part):
    frames_here, track_count, channels = query_part.shape
    anchor = jnp.einsum("fk,fkc->kc", anchor_part, query_part, preferred_element_type=jnp.float32)
    joint_query = (query_part.astype(jnp.float32) + anchor[None]).astype(jnp.bfloat16)
    shaped = (frames_here, track_count, HEADS, HEAD_DIM)
    scores = jnp.einsum(
        "fkhd,gkhd->khfg",
        joint_query.reshape(shaped),
        key_part.reshape(shaped),
        preferred_element_type=jnp.float32,
    ) * HEAD_DIM ** (-0.5)
    key_mask = jnp.transpose(seen_part) > 0
    scores = jnp.where(key_mask[:, None, None, :], scores, -jnp.inf)
    weights = jax.nn.softmax(scores, axis=-1).astype(jnp.bfloat16)
    attended = jnp.einsum(
        "khfg,gkhd->fkhd", weights, value_part.reshape(shaped), preferred_element_type=jnp.float32
    )
    return attended.astype(jnp.bfloat16).reshape(frames_here, track_count, channels)


def on_device(
    pixels,
    gru_state,
    tokens,
    visible,
    query_frame,
    pixel_query,
    pixel_key,
    pixel_value,
    pixel_out,
    time_query,
    time_key,
    time_value,
    time_out,
    gru_gates,
    gru_candidate,
):
    frame_pos = lax.axis_index("frame")
    frames = lax.axis_size("frame")
    channels = tokens.shape[2]
    half_tracks = tokens.shape[1]
    per_device = half_tracks // frames
    band_rows = pixels.shape[1]
    columns = pixels.shape[2]
    local_tokens = tokens[0]
    seen_mask = visible[0].astype(jnp.bfloat16)
    anchor_mask = (query_frame == frame_pos).astype(jnp.bfloat16)
    seen_split = seen_mask.reshape(1, frames, per_device)
    anchor_split = anchor_mask.reshape(1, frames, per_device)
    token_part = lax.all_to_all(
        local_tokens.reshape(1, frames, per_device, channels),
        "frame",
        split_axis=1,
        concat_axis=0,
        tiled=True,
    )
    seen_part = lax.all_to_all(seen_split, "frame", split_axis=1, concat_axis=0, tiled=True)
    anchor_part = lax.all_to_all(anchor_split, "frame", split_axis=1, concat_axis=0, tiled=True)
    token_rows = token_part[:, 0]
    frames_here, track_count, width_here = token_rows.shape
    flat_rows = token_rows.reshape(frames_here * track_count, width_here)
    outputs = []
    for weight in (time_query, time_key, time_value):
        outputs.append(
            jnp.dot(flat_rows, weight, preferred_element_type=jnp.float32)
            .astype(jnp.bfloat16)
            .reshape(frames_here, track_count, width_here)
        )
    result = temporal_core(outputs[0], outputs[1], outputs[2], seen_part[:, 0], anchor_part[:, 0])
    track_result = result[:, None]
    flat_pixels = pixels[0].reshape(band_rows * columns, channels)
    queries = jnp.dot(flat_pixels, pixel_query, preferred_element_type=jnp.float32).astype(
        jnp.bfloat16
    )
    key_local = jnp.dot(local_tokens, pixel_key, preferred_element_type=jnp.float32).astype(
        jnp.bfloat16
    )
    value_local = jnp.dot(local_tokens, pixel_value, preferred_element_type=jnp.float32).astype(
        jnp.bfloat16
    )
    key_rows, value_rows, seen_all = (
        lax.all_gather(key_local, "band", axis=0, tiled=True),
        lax.all_gather(value_local, "band", axis=0, tiled=True),
        lax.all_gather(seen_mask, "band", axis=0, tiled=True),
    )
    attended = attend_heads(queries, key_rows, value_rows, seen_all > 0)
    context = (
        jnp.dot(attended, pixel_out, preferred_element_type=jnp.float32)
        .astype(jnp.bfloat16)
        .reshape(band_rows, columns, GRU_WIDTH)
    )
    returned = lax.all_to_all(track_result, "frame", split_axis=0, concat_axis=1, tiled=True)
    returned_rows = returned.reshape(half_tracks, channels)
    track_update = jnp.dot(returned_rows, time_out, preferred_element_type=jnp.float32)
    track_out = (local_tokens.astype(jnp.float32) + track_update).astype(jnp.bfloat16)[None]
    state_now = gru_state[0]
    for iteration in range(ITERS):
        combined = jnp.concatenate([state_now, context], axis=-1)
        padded = with_halo(combined, (("band", 0),), 1)
        gate_terms = conv_rows(padded, gru_gates, band_rows, columns)
        update = jax.nn.sigmoid(gate_terms[:, :GRU_WIDTH])
        reset_gate = jax.nn.sigmoid(gate_terms[:, GRU_WIDTH:])
        state_flat = state_now.reshape(band_rows * columns, GRU_WIDTH).astype(jnp.float32)
        reset_state = (
            (reset_gate * state_flat).astype(jnp.bfloat16).reshape(band_rows, columns, GRU_WIDTH)
        )
        mixed_in = jnp.concatenate([reset_state, context], axis=-1)
        padded_mix = with_halo(mixed_in, (("band", 0),), 1)
        candidate = jnp.tanh(conv_rows(padded_mix, gru_candidate, band_rows, columns))
        state_now = (
            ((1.0 - update) * state_flat + update * candidate)
            .astype(jnp.bfloat16)
            .reshape(band_rows, columns, GRU_WIDTH)
        )
    refined_state = state_now[None]
    return (refined_state, track_out)


def solution(mesh):
    placed = (
        P(("clip", "frame"), "band", None, None),
        P(("clip", "frame"), "band", None, None),
        P(("clip", "frame"), "band", None),
        P(("clip", "frame"), "band"),
        P(("clip", "band")),
        P(),
        P(),
        P(),
        P(),
        P(),
        P(),
        P(),
        P(),
        P(),
        P(),
    )
    return jax.shard_map(
        on_device,
        mesh=mesh,
        in_specs=placed,
        out_specs=(P(("clip", "frame"), "band", None, None), P(("clip", "frame"), "band", None)),
        check_vma=False,
    )
```

profile of v0, /device:TPU:0, one launch (start us, length us, event | category | flops | bytes accessed | tf_op | source)
XLA Modules:
  0.0 105.7 jit_solution(6565268605685878097)
XLA Ops:
  2.7 2.3 %all_gather.10 = bf16[1024,256]{1,0:T(8,128)(2,1)S(1)} all-gather(bf16[512,256]{1,0:T(8,128)(2,1)S(1)} %convolution_convert_fusion.5), channel_id=1, replica_groups=mesh['clip'=2,'frame'=8,'band'=2] {'band'}, dimensions={0}, use_global_device_ids=true | all-gather | bytes 786432 | tf_op jit(solution)/shard_map/all_gather | solution.py:145
  5.0 1.9 %all-gather = bf16[1,1024]{1,0:T(2,128)(2,1)S(1)} all-gather(bf16[1,512]{1,0:T(2,128)(2,1)S(1)} %convert_element_type.112), channel_id=2, replica_groups=mesh['clip'=2,'frame'=8,'band'=2] {'band'}, dimensions={1}, use_global_device_ids=true | all-gather | bytes 3072 | tf_op jit(solution)/shard_map/all_gather | solution.py:147
  12.1 2.2 %all_gather.11 = bf16[1024,256]{1,0:T(8,128)(2,1)S(1)} all-gather(bf16[512,256]{1,0:T(8,128)(2,1)S(1)} %convolution_convert_fusion.4), channel_id=1, replica_groups=mesh['clip'=2,'frame'=8,'band'=2] {'band'}, dimensions={0}, use_global_device_ids=true | all-gather | bytes 786432 | tf_op jit(solution)/shard_map/all_gather | solution.py:146
  21.1 2.4 %collective-permute-start = (bf16[1,32,256]{2,1,0:T(8,128)(2,1)S(1)}, bf16[1,32,256]{2,1,0:T(8,128)(2,1)S(1)}, u32[]{:S(2)}, u32[]{:S(2)}) collective-permute-start(bf16[1,32,256]{2,1,0:T(8,128)(2,1)S(1)} %get-tuple-element.42), channel_id=1, source_target_pairs={{0,1},{2,3},{4,5},{6,7},{8,9},{10,11},{12,13},{14,15},{16,17},{18,... | collective-permute-start | bytes 49160 | tf_op jit(solution)/shard_map/ppermute | solution.py:19
  23.5 1.3 %collective-permute-start.1 = (bf16[1,32,256]{2,1,0:T(8,128)(2,1)S(1)}, bf16[1,32,256]{2,1,0:T(8,128)(2,1)S(1)}, u32[]{:S(2)}, u32[]{:S(2)}) collective-permute-start(bf16[1,32,256]{2,1,0:T(8,128)(2,1)S(1)} %get-tuple-element.2), channel_id=1, source_target_pairs={{1,0},{3,2},{5,4},{7,6},{9,8},{11,10},{13,12},{15,14},{17,16},{19,... | collective-permute-start | bytes 49160 | tf_op jit(solution)/shard_map/ppermute | solution.py:20
  25.5 7.0 %all-to-all-start.2 = ((bf16[1,8,64]{2,0,1:T(2,128)(2,1)}), bf16[1,8,64]{2,0,1:T(2,128)(2,1)S(1)}, u32[]{:S(2)}, u32[]{:S(2)}) async-start(bf16[1,8,64]{2,0,1:T(2,128)(2,1)} %reshape.250), calls=%async_computation.2 | async-start | bytes 8192 | tf_op jit(solution)/shard_map/all_to_all | solution.py:121
  34.5 2.7 %collective-permute-start.2 = (bf16[1,32,256]{2,1,0:T(8,128)(2,1)S(1)}, bf16[1,32,256]{2,1,0:T(8,128)(2,1)S(1)}, u32[]{:S(2)}, u32[]{:S(2)}) collective-permute-start(bf16[1,32,256]{2,1,0:T(8,128)(2,1)S(1)} %get-tuple-element.40), channel_id=1, source_target_pairs={{0,1},{2,3},{4,5},{6,7},{8,9},{10,11},{12,13},{14,15},{16,17},{18,... | collective-permute-start | bytes 49160 | tf_op jit(solution)/shard_map/ppermute | solution.py:19
  37.2 1.3 %collective-permute-start.3 = (bf16[1,32,256]{2,1,0:T(8,128)(2,1)S(1)}, bf16[1,32,256]{2,1,0:T(8,128)(2,1)S(1)}, u32[]{:S(2)}, u32[]{:S(2)}) collective-permute-start(bf16[1,32,256]{2,1,0:T(8,128)(2,1)S(1)} %get-tuple-element.41), channel_id=1, source_target_pairs={{1,0},{3,2},{5,4},{7,6},{9,8},{11,10},{13,12},{15,14},{17,16},{19,... | collective-permute-start | bytes 49160 | tf_op jit(solution)/shard_map/ppermute | solution.py:20
  42.1 2.1 %collective-permute-start.4 = (bf16[1,32,256]{2,1,0:T(8,128)(2,1)S(1)}, bf16[1,32,256]{2,1,0:T(8,128)(2,1)S(1)}, u32[]{:S(2)}, u32[]{:S(2)}) collective-permute-start(bf16[1,32,256]{2,1,0:T(8,128)(2,1)S(1)} %get-tuple-element.38), channel_id=1, source_target_pairs={{0,1},{2,3},{4,5},{6,7},{8,9},{10,11},{12,13},{14,15},{16,17},{18,... | collective-permute-start | bytes 49160 | tf_op jit(solution)/shard_map/ppermute | solution.py:19
  44.2 1.3 %collective-permute-start.5 = (bf16[1,32,256]{2,1,0:T(8,128)(2,1)S(1)}, bf16[1,32,256]{2,1,0:T(8,128)(2,1)S(1)}, u32[]{:S(2)}, u32[]{:S(2)}) collective-permute-start(bf16[1,32,256]{2,1,0:T(8,128)(2,1)S(1)} %get-tuple-element.39), channel_id=1, source_target_pairs={{1,0},{3,2},{5,4},{7,6},{9,8},{11,10},{13,12},{15,14},{17,16},{19,... | collective-permute-start | bytes 49160 | tf_op jit(solution)/shard_map/ppermute | solution.py:20
  45.5 5.7 %all-to-all-start.1 = ((bf16[1,8,64]{2,0,1:T(2,128)(2,1)}), bf16[1,8,64]{2,0,1:T(2,128)(2,1)S(1)}, u32[]{:S(2)}, u32[]{:S(2)}) async-start(bf16[1,8,64]{2,0,1:T(2,128)(2,1)} %convert_element_type.145), calls=%async_computation.1 | async-start | bytes 8192 | tf_op jit(solution)/shard_map/all_to_all | solution.py:120
  53.9 2.7 %collective-permute-start.6 = (bf16[1,32,256]{2,1,0:T(8,128)(2,1)S(1)}, bf16[1,32,256]{2,1,0:T(8,128)(2,1)S(1)}, u32[]{:S(2)}, u32[]{:S(2)}) collective-permute-start(bf16[1,32,256]{2,1,0:T(8,128)(2,1)S(1)} %get-tuple-element.36), channel_id=1, source_target_pairs={{0,1},{2,3},{4,5},{6,7},{8,9},{10,11},{12,13},{14,15},{16,17},{18,... | collective-permute-start | bytes 49160 | tf_op jit(solution)/shard_map/ppermute | solution.py:19
  56.6 1.3 %collective-permute-start.7 = (bf16[1,32,256]{2,1,0:T(8,128)(2,1)S(1)}, bf16[1,32,256]{2,1,0:T(8,128)(2,1)S(1)}, u32[]{:S(2)}, u32[]{:S(2)}) collective-permute-start(bf16[1,32,256]{2,1,0:T(8,128)(2,1)S(1)} %get-tuple-element.37), channel_id=1, source_target_pairs={{1,0},{3,2},{5,4},{7,6},{9,8},{11,10},{13,12},{15,14},{17,16},{19,... | collective-permute-start | bytes 49160 | tf_op jit(solution)/shard_map/ppermute | solution.py:20
  58.0 5.7 %all-to-all-start = ((bf16[1,8,64,256]{3,2,0,1:T(8,128)(2,1)}), bf16[1,8,64,256]{3,2,0,1:T(8,128)(2,1)S(1)}, u32[]{:S(2)}, u32[]{:S(2)}) async-start(bf16[1,8,64,256]{3,2,0,1:T(8,128)(2,1)} %bitcast.61), calls=%async_computation | async-start | bytes 524288 | tf_op jit(solution)/shard_map/all_to_all | solution.py:113
  67.1 6.8 %all-to-all-done = bf16[1,8,64,256]{3,2,0,1:T(8,128)(2,1)S(1)} async-done(((bf16[1,8,64,256]{3,2,0,1:T(8,128)(2,1)}), bf16[1,8,64,256]{3,2,0,1:T(8,128)(2,1)S(1)}, u32[]{:S(2)}, u32[]{:S(2)}) %all-to-all-start) | async-done | bytes 262176 | tf_op jit(solution)/shard_map/all_to_all | solution.py:113
  74.8 1.8 %copy.70 = bf16[8,64,8,32]{3,0,2,1:T(8,128)(2,1)S(1)} copy(bf16[8,64,8,32]{1,0,3,2:T(8,128)(2,1)S(1)} %add_convert_fusion) | data formatting | bytes 524288 | tf_op jit(solution)/shard_map/convert_element_type | solution.py:67
  77.2 2.7 %copy.71 = bf16[8,64,8,32]{3,0,2,1:T(8,128)(2,1)} copy(bf16[8,64,8,32]{1,0,3,2:T(8,128)(2,1)S(1)} %reshape_reshape.7) | data formatting | bytes 524288 | tf_op jit(solution)/shard_map/reshape;reshape | solution.py:72
  79.9 1.9 %fusion.205 = f32[64,8,8,8]{2,3,1,0:T(8,128)S(1)} fusion(bf16[8,64,8,32]{3,0,2,1:T(8,128)(2,1)S(1)} %copy.70, bf16[8,64,8,32]{3,0,2,1:T(8,128)(2,1)} %copy.71), kind=kOutput, calls=%fused_computation.340 | convolution fusion | flops 2097152 | bytes 655360 | tf_op jit(solution)/shard_map/fkhd,gkhd->khfg/dot_general | solution.py:69
  84.2 1.6 %copy.74 = bf16[64,8,8,8]{3,2,1,0:T(8,128)(2,1)S(1)} copy(bf16[64,8,8,8]{0,3,2,1:T(8,128)(2,1)S(1)} %divide_convert_fusion.16) | data formatting | bytes 131072 | tf_op jit(solution)/shard_map/convert_element_type | solution.py:77
  86.5 1.8 %copy.73 = bf16[8,64,8,32]{3,0,2,1:T(8,128)(2,1)S(1)} copy(bf16[8,64,8,32]{1,0,3,2:T(8,128)(2,1)S(1)} %reshape_reshape.6) | data formatting | bytes 524288 | tf_op jit(solution)/shard_map/reshape;reshape | solution.py:79
  91.0 3.6 %all-to-all-start.3 = ((bf16[8,1,64,256]{3,2,1,0:T(8,128)(2,1)}), bf16[8,1,64,256]{3,2,1,0:T(8,128)(2,1)S(1)}, u32[]{:S(2)}, u32[]{:S(2)}) async-start(bf16[8,1,64,256]{3,2,1,0:T(8,128)(2,1)} %copy.76), calls=%async_computation.3 | async-start | bytes 524288 | tf_op jit(solution)/shard_map/all_to_all | solution.py:155
  95.7 1.7 %fusion.24 = bf16[256,128]{1,0:T(8,128)(2,1)} fusion(f32[256,128]{1,0:T(8,128)S(1)} %fusion.138, f32[256,128]{1,0:T(8,128)S(1)} %copy-done.16, bf16[256,256]{1,0:T(8,128)(2,1)S(1)} %bitcast.277, bf16[256,128]{1,0:T(8,128)(2,1)S(1)} %copy-done.5, f32[256,256]{1,0:T(8,128)S(1)} %copy-done.7, bf16[3,3,256,128]{3,2,1,0:T(8,128)(2,1)} %param.29), kind=kOutput, calls=%fused_computation.68 | convolution fusion | flops 17137664 | bytes 720896 | tf_op jit(solution)/shard_map/dot_general | solution.py:56
  97.4 6.5 %all-to-all-done.3 = bf16[8,1,64,256]{3,2,1,0:T(8,128)(2,1)S(1)} async-done(((bf16[8,1,64,256]{3,2,1,0:T(8,128)(2,1)}), bf16[8,1,64,256]{3,2,1,0:T(8,128)(2,1)S(1)}, u32[]{:S(2)}, u32[]{:S(2)}) %all-to-all-start.3) | async-done | bytes 262176 | tf_op jit(solution)/shard_map/all_to_all | solution.py:155
  103.9 1.9 %fusion.12 = bf16[1,512,256]{2,1,0:T(8,128)(2,1)} fusion(bf16[512,256]{1,0:T(8,128)(2,1)S(1)} %bitcast.244, bf16[256,256]{1,0:T(8,128)(2,1)S(1)} %copy-done.15, bf16[1,512,256]{2,1,0:T(8,128)(2,1)} %param.17), kind=kOutput, calls=%fused_computation.27 | convolution fusion | flops 67502080 | bytes 917504 | tf_op jit(solution)/shard_map/dot_general | solution.py:157
  (159 shorter events, 34.1 us)
Async XLA Ops:
  0.7 6.3 %copy-start.9 = (bf16[1,8,32,256]{3,2,1,0:T(8,128)(2,1)S(1)}, bf16[1,8,32,256]{3,2,1,0:T(8,128)(2,1)}, u32[]{:S(2)}) copy-start(bf16[1,8,32,256]{3,2,1,0:T(8,128)(2,1)} %param.15) | copy-start | bytes 393220
  0.7 6.3 %copy-start.10 = (bf16[256,256]{1,0:T(8,128)(2,1)S(1)}, bf16[256,256]{1,0:T(8,128)(2,1)}, u32[]{:S(2)}) copy-start(bf16[256,256]{1,0:T(8,128)(2,1)} %param.20) | copy-start | bytes 393220
  20.8 11.8 %copy-start.1 = (bf16[3,3,256,256]{3,2,1,0:T(8,128)(2,1)S(1)}, bf16[3,3,256,256]{3,2,1,0:T(8,128)(2,1)}, u32[]{:S(2)}) copy-start(bf16[3,3,256,256]{3,2,1,0:T(8,128)(2,1)} %param.28) | copy-start | bytes 3538948
  21.1 11.4 %collective-permute-start = (bf16[1,32,256]{2,1,0:T(8,128)(2,1)S(1)}, bf16[1,32,256]{2,1,0:T(8,128)(2,1)S(1)}, u32[]{:S(2)}, u32[]{:S(2)}) collective-permute-start(bf16[1,32,256]{2,1,0:T(8,128)(2,1)S(1)} %get-tuple-element.42), channel_id=1, source_target_pairs={{0,1},{2,3},{4,5},{6,7},{8,9},{10,11},{12,13},{14,15},{16,17},{18,... | collective-permute-start | bytes 49160 | tf_op jit(solution)/shard_map/ppermute | solution.py:19
  23.5 9.0 %collective-permute-start.1 = (bf16[1,32,256]{2,1,0:T(8,128)(2,1)S(1)}, bf16[1,32,256]{2,1,0:T(8,128)(2,1)S(1)}, u32[]{:S(2)}, u32[]{:S(2)}) collective-permute-start(bf16[1,32,256]{2,1,0:T(8,128)(2,1)S(1)} %get-tuple-element.2), channel_id=1, source_target_pairs={{1,0},{3,2},{5,4},{7,6},{9,8},{11,10},{13,12},{15,14},{17,16},{19,... | collective-permute-start | bytes 49160 | tf_op jit(solution)/shard_map/ppermute | solution.py:20
  25.5 20.0 %all-to-all-start.2 = ((bf16[1,8,64]{2,0,1:T(2,128)(2,1)}), bf16[1,8,64]{2,0,1:T(2,128)(2,1)S(1)}, u32[]{:S(2)}, u32[]{:S(2)}) async-start(bf16[1,8,64]{2,0,1:T(2,128)(2,1)} %reshape.250), calls=%async_computation.2 | async-start | bytes 8192 | tf_op jit(solution)/shard_map/all_to_all | solution.py:121
  34.2 6.3 %copy-start.2 = (bf16[3,3,256,128]{3,2,1,0:T(8,128)(2,1)S(1)}, bf16[3,3,256,128]{3,2,1,0:T(8,128)(2,1)}, u32[]{:S(2)}) copy-start(bf16[3,3,256,128]{3,2,1,0:T(8,128)(2,1)} %param.29) | copy-start | bytes 1769476
  34.5 4.8 %collective-permute-start.2 = (bf16[1,32,256]{2,1,0:T(8,128)(2,1)S(1)}, bf16[1,32,256]{2,1,0:T(8,128)(2,1)S(1)}, u32[]{:S(2)}, u32[]{:S(2)}) collective-permute-start(bf16[1,32,256]{2,1,0:T(8,128)(2,1)S(1)} %get-tuple-element.40), channel_id=1, source_target_pairs={{0,1},{2,3},{4,5},{6,7},{8,9},{10,11},{12,13},{14,15},{16,17},{18,... | collective-permute-start | bytes 49160 | tf_op jit(solution)/shard_map/ppermute | solution.py:19
  37.2 3.1 %collective-permute-start.3 = (bf16[1,32,256]{2,1,0:T(8,128)(2,1)S(1)}, bf16[1,32,256]{2,1,0:T(8,128)(2,1)S(1)}, u32[]{:S(2)}, u32[]{:S(2)}) collective-permute-start(bf16[1,32,256]{2,1,0:T(8,128)(2,1)S(1)} %get-tuple-element.41), channel_id=1, source_target_pairs={{1,0},{3,2},{5,4},{7,6},{9,8},{11,10},{13,12},{15,14},{17,16},{19,... | collective-permute-start | bytes 49160 | tf_op jit(solution)/shard_map/ppermute | solution.py:20
  42.1 11.1 %copy-start.4 = (bf16[256,128]{1,0:T(8,128)(2,1)}, bf16[256,128]{1,0:T(8,128)(2,1)S(1)}, u32[]{:S(2)}) copy-start(bf16[256,128]{1,0:T(8,128)(2,1)S(1)} %fusion.25) | copy-start | bytes 196612
  42.1 9.1 %collective-permute-start.4 = (bf16[1,32,256]{2,1,0:T(8,128)(2,1)S(1)}, bf16[1,32,256]{2,1,0:T(8,128)(2,1)S(1)}, u32[]{:S(2)}, u32[]{:S(2)}) collective-permute-start(bf16[1,32,256]{2,1,0:T(8,128)(2,1)S(1)} %get-tuple-element.38), channel_id=1, source_target_pairs={{0,1},{2,3},{4,5},{6,7},{8,9},{10,11},{12,13},{14,15},{16,17},{18,... | collective-permute-start | bytes 49160 | tf_op jit(solution)/shard_map/ppermute | solution.py:19
  44.2 7.0 %collective-permute-start.5 = (bf16[1,32,256]{2,1,0:T(8,128)(2,1)S(1)}, bf16[1,32,256]{2,1,0:T(8,128)(2,1)S(1)}, u32[]{:S(2)}, u32[]{:S(2)}) collective-permute-start(bf16[1,32,256]{2,1,0:T(8,128)(2,1)S(1)} %get-tuple-element.39), channel_id=1, source_target_pairs={{1,0},{3,2},{5,4},{7,6},{9,8},{11,10},{13,12},{15,14},{17,16},{19,... | collective-permute-start | bytes 49160 | tf_op jit(solution)/shard_map/ppermute | solution.py:20
  45.5 12.4 %all-to-all-start.1 = ((bf16[1,8,64]{2,0,1:T(2,128)(2,1)}), bf16[1,8,64]{2,0,1:T(2,128)(2,1)S(1)}, u32[]{:S(2)}, u32[]{:S(2)}) async-start(bf16[1,8,64]{2,0,1:T(2,128)(2,1)} %convert_element_type.145), calls=%async_computation.1 | async-start | bytes 8192 | tf_op jit(solution)/shard_map/all_to_all | solution.py:120
  53.9 9.8 %collective-permute-start.6 = (bf16[1,32,256]{2,1,0:T(8,128)(2,1)S(1)}, bf16[1,32,256]{2,1,0:T(8,128)(2,1)S(1)}, u32[]{:S(2)}, u32[]{:S(2)}) collective-permute-start(bf16[1,32,256]{2,1,0:T(8,128)(2,1)S(1)} %get-tuple-element.36), channel_id=1, source_target_pairs={{0,1},{2,3},{4,5},{6,7},{8,9},{10,11},{12,13},{14,15},{16,17},{18,... | collective-permute-start | bytes 49160 | tf_op jit(solution)/shard_map/ppermute | solution.py:19
  56.6 7.1 %collective-permute-start.7 = (bf16[1,32,256]{2,1,0:T(8,128)(2,1)S(1)}, bf16[1,32,256]{2,1,0:T(8,128)(2,1)S(1)}, u32[]{:S(2)}, u32[]{:S(2)}) collective-permute-start(bf16[1,32,256]{2,1,0:T(8,128)(2,1)S(1)} %get-tuple-element.37), channel_id=1, source_target_pairs={{1,0},{3,2},{5,4},{7,6},{9,8},{11,10},{13,12},{15,14},{17,16},{19,... | collective-permute-start | bytes 49160 | tf_op jit(solution)/shard_map/ppermute | solution.py:20
  58.0 15.9 %all-to-all-start = ((bf16[1,8,64,256]{3,2,0,1:T(8,128)(2,1)}), bf16[1,8,64,256]{3,2,0,1:T(8,128)(2,1)S(1)}, u32[]{:S(2)}, u32[]{:S(2)}) async-start(bf16[1,8,64,256]{3,2,0,1:T(8,128)(2,1)} %bitcast.61), calls=%async_computation | async-start | bytes 524288 | tf_op jit(solution)/shard_map/all_to_all | solution.py:113
  65.5 8.3 %copy-start.12 = (bf16[256,256]{1,0:T(8,128)(2,1)S(1)}, bf16[256,256]{1,0:T(8,128)(2,1)}, u32[]{:S(2)}) copy-start(bf16[256,256]{1,0:T(8,128)(2,1)} %param.24) | copy-start | bytes 393220
  88.9 5.8 %copy-start.8 = (bf16[8,32,256]{2,1,0:T(8,128)(2,1)S(1)}, bf16[8,32,256]{2,1,0:T(8,128)(2,1)}, u32[]{:S(2)}) copy-start(bf16[8,32,256]{2,1,0:T(8,128)(2,1)} %get-tuple-element.8) | copy-start | bytes 393220
  90.1 5.6 %copy-start.5 = (bf16[256,128]{1,0:T(8,128)(2,1)S(1)}, bf16[256,128]{1,0:T(8,128)(2,1)}, u32[]{:S(2)}) copy-start(bf16[256,128]{1,0:T(8,128)(2,1)} %copy-done.4) | copy-start | bytes 196612
  90.1 5.6 %copy-start.7 = (f32[256,256]{1,0:T(8,128)S(1)}, f32[256,256]{1,0:T(8,128)}, u32[]{:S(2)}) copy-start(f32[256,256]{1,0:T(8,128)} %copy-done.6) | copy-start | bytes 786436
  90.1 5.6 %copy-start.16 = (f32[256,128]{1,0:T(8,128)S(1)}, f32[256,128]{1,0:T(8,128)}, u32[]{:S(2)}) copy-start(f32[256,128]{1,0:T(8,128)} %convolution_add_fusion.16) | copy-start | bytes 393220
  90.1 5.6 %copy-start.17 = (bf16[8,32,256]{2,1,0:T(8,128)(2,1)S(1)}, bf16[8,32,256]{2,1,0:T(8,128)(2,1)}, u32[]{:S(2)}) copy-start(bf16[8,32,256]{2,1,0:T(8,128)(2,1)} %get-tuple-element.28) | copy-start | bytes 393220
  90.1 13.7 %copy-start.15 = (bf16[256,256]{1,0:T(8,128)(2,1)S(1)}, bf16[256,256]{1,0:T(8,128)(2,1)}, u32[]{:S(2)}) copy-start(bf16[256,256]{1,0:T(8,128)(2,1)} %param.27) | copy-start | bytes 393220
  91.0 12.8 %all-to-all-start.3 = ((bf16[8,1,64,256]{3,2,1,0:T(8,128)(2,1)}), bf16[8,1,64,256]{3,2,1,0:T(8,128)(2,1)S(1)}, u32[]{:S(2)}, u32[]{:S(2)}) async-start(bf16[8,1,64,256]{3,2,1,0:T(8,128)(2,1)} %copy.76), calls=%async_computation.3 | async-start | bytes 524288 | tf_op jit(solution)/shard_map/all_to_all | solution.py:155
  (9 other events, 18.2 us)
where the time goes:
time: 107 us; the launch traced here: 106 us
  starting transfers between devices  37.2 us (35%)
  matrix products  24.6 us (23%)
  local copies, waits for them, and re-layouts  16.6 us (16%)
  waiting for transfers between devices  14.3 us (13%)
  blocking collectives  6.35 us (6%)
  other arithmetic  5.05 us (5%)
  between operations  1.63 us (2%)
    ppermute x4, starting transfers between devices, with_halo(): before = lax.ppermute(last, axis, up)  9.94 us
    dot_general x36, matrix products, conv_rows(): jnp.dot(window.reshape(rows * columns, -1), weight[row_shift, col_shift],...  9.4 us
    all_to_all x1, starting transfers between devices, on_device(): lax.all_to_all(anchor_split, 'frame', split_axis=1, concat_axis=0, tiled=...  6.98 us
    all_to_all x1, waiting for transfers between devices, on_device(): lax.all_to_all(local_tokens.reshape(1, frames, per_device, channels), 'fr...  6.77 us
    all_to_all x1, waiting for transfers between devices, on_device(): lax.all_to_all(track_result, 'frame', split_axis=0, concat_axis=1, tiled=...  6.47 us
    all_to_all x1, starting transfers between devices, on_device(): lax.all_to_all(local_tokens.reshape(1, frames, per_device, channels), 'fr...  5.72 us
    all_to_all x1, starting transfers between devices, on_device(): lax.all_to_all(seen_split, 'frame', split_axis=1, concat_axis=0, tiled=True)  5.72 us
    ppermute x4, starting transfers between devices, with_halo(): after = lax.ppermute(first, axis, down)  5.17 us
  transfers between devices with their start and end apart: 12, of which 3 were waited for; matrix products, arithmetic and copies ran while one was open for 12% of the time, Pallas kernels for 0%

commit v1 on v0

--- a/solution.py
+++ b/solution.py
@@ -7,6 +7,17 @@
 HEAD_DIM = 32
 GRU_WIDTH = 128
 ITERS = 2
+
+
+def split_up(array, dim, devices):
+    before, after = (array.shape[:dim], array.shape[dim + 1 :])
+    return jnp.moveaxis(array.reshape(*before, devices, -1, *after), dim, 0)
+
+
+def in_order(parts, dim):
+    parts = jnp.moveaxis(parts, 0, dim)
+    shape = parts.shape
+    return parts.reshape(*shape[:dim], shape[dim] * shape[dim + 1], *shape[dim + 2 :])
 
 
 def with_halo(x, sides, width):
@@ -117,7 +128,14 @@
         concat_axis=0,
         tiled=True,
     )
-    seen_part = lax.all_to_all(seen_split, "frame", split_axis=1, concat_axis=0, tiled=True)
+    count, index = (lax.axis_size("frame"), lax.axis_index("frame"))
+    parts = split_up(seen_split, 1, count)
+    outs = [parts[index]]
+    for step in range(1, count):
+        sent = parts[index ^ step]
+        outs.append(lax.ppermute(sent, "frame", [(i_2, i_2 ^ step) for i_2 in range(count)]))
+    parts = jnp.stack(outs)[index ^ jnp.arange(count)]
+    seen_part = in_order(parts, 0)
     anchor_part = lax.all_to_all(anchor_split, "frame", split_axis=1, concat_axis=0, tiled=True)
     token_rows = token_part[:, 0]
     frames_here, track_count, width_here = token_rows.shape

time: 107 us -> 118 us (1.10)
  waiting for transfers between devices: 14.3 us -> 21.2 us
  starting transfers between devices: 37.2 us -> 40.3 us
  other arithmetic: 5.05 us -> 7.19 us
    ppermute x0 -> x7, starting transfers between devices: none -> 13.9 us  [on_device(): lax.ppermute(sent, 'frame', [(i_2, i_2 ^ step) for i_2 in range(count)])]
    all_to_all x1 -> x0, starting transfers between devices: 5.72 us -> none  [on_device(): lax.all_to_all(seen_split, 'frame', split_axis=1, concat_axis=0, tiled=True)]
    ppermute x0 -> x7, waiting for transfers between devices: none -> 4.74 us  [on_device(): lax.ppermute(sent, 'frame', [(i_2, i_2 ^ step) for i_2 in range(count)])]
    ppermute x4, waiting for transfers between devices: 1.08 us -> 3.51 us  [with_halo(): after = lax.ppermute(first, axis, down)]
    ppermute x4, starting transfers between devices: 9.94 us -> 7.62 us  [with_halo(): before = lax.ppermute(last, axis, up)]
    all_to_all x1, starting transfers between devices: 5.72 us -> 3.61 us  [on_device(): lax.all_to_all(local_tokens.reshape(1, frames, per_device, channels), 'fr...]
    convert_element_type x2, other arithmetic: 0.03 us -> 1.47 us  [on_device(): seen_mask = visible[0].astype(jnp.bfloat16)]
  transfers between devices with their start and end apart: 12 -> 18, of which waited for: 3 -> 6; matrix products, arithmetic and copies ran while one was open for 12% -> 23% of each run, Pallas kernels for 0% -> 0%
where the time goes in v1:
time: 118 us; the launch traced here: 117 us
  starting transfers between devices  40.3 us (34%)
  matrix products  24.6 us (21%)
  waiting for transfers between devices  21.2 us (18%)
  local copies, waits for them, and re-layouts  15.8 us (13%)
  other arithmetic  7.19 us (6%)
  blocking collectives  6.19 us (5%)
  between operations  1.66 us (1%)
    ppermute x7, starting transfers between devices, on_device(): lax.ppermute(sent, 'frame', [(i_2, i_2 ^ step) for i_2 in range(count)])  13.9 us
    dot_general x36, matrix products, conv_rows(): jnp.dot(window.reshape(rows * columns, -1), weight[row_shift, col_shift],...  9.39 us
    ppermute x4, starting transfers between devices, with_halo(): before = lax.ppermute(last, axis, up)  7.62 us
    all_to_all x1, waiting for transfers between devices, on_device(): lax.all_to_all(track_result, 'frame', split_axis=0, concat_axis=1, tiled=...  6.48 us
    all_to_all x1, waiting for transfers between devices, on_device(): lax.all_to_all(local_tokens.reshape(1, frames, per_device, channels), 'fr...  6.47 us
    all_to_all x1, starting transfers between devices, on_device(): lax.all_to_all(anchor_split, 'frame', split_axis=1, concat_axis=0, tiled=...  6.22 us
    ppermute x4, starting transfers between devices, with_halo(): after = lax.ppermute(first, axis, down)  5.17 us
    ppermute x7, waiting for transfers between devices, on_device(): lax.ppermute(sent, 'frame', [(i_2, i_2 ^ step) for i_2 in range(count)])  4.74 us
  transfers between devices with their start and end apart: 18, of which 6 were waited for; matrix products, arithmetic and copies ran while one was open for 23% of the time, Pallas kernels for 0%

profile of v1, /device:TPU:0, one launch (start us, length us, event | category | flops | bytes accessed | tf_op | source)
XLA Modules:
  0.0 116.9 jit_solution(17420221626987052189)
XLA Ops:
  1.6 3.1 %collective-permute-start.8 = (bf16[1,1,64]{2,1,0:T(2,128)(2,1)S(1)}, bf16[1,1,64]{2,1,0:T(2,128)(2,1)S(1)}, u32[]{:S(2)}, u32[]{:S(2)}) collective-permute-start(bf16[1,1,64]{2,1,0:T(2,128)(2,1)S(1)} %get-tuple-element.49), channel_id=1, source_target_pairs={{0,2},{2,0},{4,6},{6,4},{8,10},{10,8},{12,14},{14,12},{1,3},{3,1},... | collective-permute-start | bytes 392 | tf_op jit(solution)/shard_map/ppermute | solution.py:136
  4.7 1.6 %collective-permute-start.9 = (bf16[1,1,64]{2,1,0:T(2,128)(2,1)S(1)}, bf16[1,1,64]{2,1,0:T(2,128)(2,1)S(1)}, u32[]{:S(2)}, u32[]{:S(2)}) collective-permute-start(bf16[1,1,64]{2,1,0:T(2,128)(2,1)S(1)} %get-tuple-element.48), channel_id=1, source_target_pairs={{0,4},{2,6},{4,0},{6,2},{8,12},{10,14},{12,8},{14,10},{1,5},{3,7},... | collective-permute-start | bytes 392 | tf_op jit(solution)/shard_map/ppermute | solution.py:136
  7.6 6.2 %all-to-all-start.1 = ((bf16[1,8,64]{2,0,1:T(2,128)(2,1)}), bf16[1,8,64]{2,0,1:T(2,128)(2,1)S(1)}, u32[]{:S(2)}, u32[]{:S(2)}) async-start(bf16[1,8,64]{2,0,1:T(2,128)(2,1)} %reshape.280), calls=%async_computation.1 | async-start | bytes 8192 | tf_op jit(solution)/shard_map/all_to_all | solution.py:139
  15.7 2.2 %all_gather.10 = bf16[1024,256]{1,0:T(8,128)(2,1)S(1)} all-gather(bf16[512,256]{1,0:T(8,128)(2,1)S(1)} %convolution_convert_fusion.5), channel_id=1, replica_groups=mesh['clip'=2,'frame'=8,'band'=2] {'band'}, dimensions={0}, use_global_device_ids=true | all-gather | bytes 786432 | tf_op jit(solution)/shard_map/all_gather | solution.py:163
  17.9 1.8 %all-gather = bf16[1,1024]{1,0:T(2,128)(2,1)S(1)} all-gather(bf16[1,512]{1,0:T(2,128)(2,1)S(1)} %convert_element_type.112), channel_id=2, replica_groups=mesh['clip'=2,'frame'=8,'band'=2] {'band'}, dimensions={1}, use_global_device_ids=true | all-gather | bytes 3072 | tf_op jit(solution)/shard_map/all_gather | solution.py:165
  24.9 2.2 %all_gather.11 = bf16[1024,256]{1,0:T(8,128)(2,1)S(1)} all-gather(bf16[512,256]{1,0:T(8,128)(2,1)S(1)} %convolution_convert_fusion.4), channel_id=1, replica_groups=mesh['clip'=2,'frame'=8,'band'=2] {'band'}, dimensions={0}, use_global_device_ids=true | all-gather | bytes 786432 | tf_op jit(solution)/shard_map/all_gather | solution.py:164
  33.9 2.2 %collective-permute-start = (bf16[1,32,256]{2,1,0:T(8,128)(2,1)S(1)}, bf16[1,32,256]{2,1,0:T(8,128)(2,1)S(1)}, u32[]{:S(2)}, u32[]{:S(2)}) collective-permute-start(bf16[1,32,256]{2,1,0:T(8,128)(2,1)S(1)} %get-tuple-element.42), channel_id=1, source_target_pairs={{0,1},{2,3},{4,5},{6,7},{8,9},{10,11},{12,13},{14,15},{16,17},{18,... | collective-permute-start | bytes 49160 | tf_op jit(solution)/shard_map/ppermute | solution.py:30
  37.4 1.8 %collective-permute-done.1 = bf16[1,32,256]{2,1,0:T(8,128)(2,1)S(1)} collective-permute-done((bf16[1,32,256]{2,1,0:T(8,128)(2,1)S(1)}, bf16[1,32,256]{2,1,0:T(8,128)(2,1)S(1)}, u32[]{:S(2)}, u32[]{:S(2)}) %collective-permute-start.1) | collective-permute-done | bytes 16416 | tf_op jit(solution)/shard_map/ppermute | solution.py:31
  41.2 2.1 %collective-permute-start.2 = (bf16[1,32,256]{2,1,0:T(8,128)(2,1)S(1)}, bf16[1,32,256]{2,1,0:T(8,128)(2,1)S(1)}, u32[]{:S(2)}, u32[]{:S(2)}) collective-permute-start(bf16[1,32,256]{2,1,0:T(8,128)(2,1)S(1)} %get-tuple-element.40), channel_id=1, source_target_pairs={{0,1},{2,3},{4,5},{6,7},{8,9},{10,11},{12,13},{14,15},{16,17},{18,... | collective-permute-start | bytes 49160 | tf_op jit(solution)/shard_map/ppermute | solution.py:30
  44.6 3.0 %collective-permute-start.11 = (bf16[1,1,64]{2,1,0:T(2,128)(2,1)S(1)}, bf16[1,1,64]{2,1,0:T(2,128)(2,1)S(1)}, u32[]{:S(2)}, u32[]{:S(2)}) collective-permute-start(bf16[1,1,64]{2,1,0:T(2,128)(2,1)S(1)} %get-tuple-element.46), channel_id=1, source_target_pairs={{0,8},{2,10},{4,12},{6,14},{8,0},{10,2},{12,4},{14,6},{1,9},{3,11}... | collective-permute-start | bytes 392 | tf_op jit(solution)/shard_map/ppermute | solution.py:136
  49.0 3.3 %collective-permute-start.13 = (bf16[1,1,64]{2,1,0:T(2,128)(2,1)S(1)}, bf16[1,1,64]{2,1,0:T(2,128)(2,1)S(1)}, u32[]{:S(2)}, u32[]{:S(2)}) collective-permute-start(bf16[1,1,64]{2,1,0:T(2,128)(2,1)S(1)} %get-tuple-element.44), channel_id=1, source_target_pairs={{0,12},{2,14},{4,8},{6,10},{8,4},{10,6},{12,0},{14,2},{1,13},{3,15... | collective-permute-start | bytes 392 | tf_op jit(solution)/shard_map/ppermute | solution.py:136
  54.4 4.2 %collective-permute-done.14 = bf16[1,1,64]{2,1,0:T(2,128)(2,1)S(1)} collective-permute-done((bf16[1,1,64]{2,1,0:T(2,128)(2,1)S(1)}, bf16[1,1,64]{2,1,0:T(2,128)(2,1)S(1)}, u32[]{:S(2)}, u32[]{:S(2)}) %collective-permute-start.14) | collective-permute-done | bytes 160 | tf_op jit(solution)/shard_map/ppermute | solution.py:136
  63.6 1.8 %collective-permute-done.5 = bf16[1,32,256]{2,1,0:T(8,128)(2,1)S(1)} collective-permute-done((bf16[1,32,256]{2,1,0:T(8,128)(2,1)S(1)}, bf16[1,32,256]{2,1,0:T(8,128)(2,1)S(1)}, u32[]{:S(2)}, u32[]{:S(2)}) %collective-permute-start.5) | collective-permute-done | bytes 16416 | tf_op jit(solution)/shard_map/ppermute | solution.py:31
  68.0 2.1 %collective-permute-start.6 = (bf16[1,32,256]{2,1,0:T(8,128)(2,1)S(1)}, bf16[1,32,256]{2,1,0:T(8,128)(2,1)S(1)}, u32[]{:S(2)}, u32[]{:S(2)}) collective-permute-start(bf16[1,32,256]{2,1,0:T(8,128)(2,1)S(1)} %get-tuple-element.36), channel_id=1, source_target_pairs={{0,1},{2,3},{4,5},{6,7},{8,9},{10,11},{12,13},{14,15},{16,17},{18,... | collective-permute-start | bytes 49160 | tf_op jit(solution)/shard_map/ppermute | solution.py:30
  71.4 3.6 %all-to-all-start = ((bf16[1,8,64,256]{3,2,0,1:T(8,128)(2,1)}), bf16[1,8,64,256]{3,2,0,1:T(8,128)(2,1)S(1)}, u32[]{:S(2)}, u32[]{:S(2)}) async-start(bf16[1,8,64,256]{3,2,0,1:T(8,128)(2,1)} %bitcast.61), calls=%async_computation | async-start | bytes 524288 | tf_op jit(solution)/shard_map/all_to_all | solution.py:124
  78.4 6.5 %all-to-all-done = bf16[1,8,64,256]{3,2,0,1:T(8,128)(2,1)S(1)} async-done(((bf16[1,8,64,256]{3,2,0,1:T(8,128)(2,1)}), bf16[1,8,64,256]{3,2,0,1:T(8,128)(2,1)S(1)}, u32[]{:S(2)}, u32[]{:S(2)}) %all-to-all-start) | async-done | bytes 262176 | tf_op jit(solution)/shard_map/all_to_all | solution.py:124
  85.8 1.8 %copy.108 = bf16[8,64,8,32]{3,0,2,1:T(8,128)(2,1)S(1)} copy(bf16[8,64,8,32]{1,0,3,2:T(8,128)(2,1)S(1)} %add_convert_fusion) | data formatting | bytes 524288 | tf_op jit(solution)/shard_map/convert_element_type | solution.py:78
  88.3 2.7 %copy.109 = bf16[8,64,8,32]{3,0,2,1:T(8,128)(2,1)} copy(bf16[8,64,8,32]{1,0,3,2:T(8,128)(2,1)S(1)} %reshape_reshape.7) | data formatting | bytes 524288 | tf_op jit(solution)/shard_map/reshape;reshape | solution.py:83
  91.0 1.9 %fusion.213 = f32[64,8,8,8]{2,3,1,0:T(8,128)S(1)} fusion(bf16[8,64,8,32]{3,0,2,1:T(8,128)(2,1)S(1)} %copy.108, bf16[8,64,8,32]{3,0,2,1:T(8,128)(2,1)} %copy.109), kind=kOutput, calls=%fused_computation.359 | convolution fusion | flops 2097152 | bytes 655360 | tf_op jit(solution)/shard_map/fkhd,gkhd->khfg/dot_general | solution.py:80
  97.5 1.8 %copy.111 = bf16[8,64,8,32]{3,0,2,1:T(8,128)(2,1)S(1)} copy(bf16[8,64,8,32]{1,0,3,2:T(8,128)(2,1)S(1)} %reshape_reshape.6) | data formatting | bytes 524288 | tf_op jit(solution)/shard_map/reshape;reshape | solution.py:90
  102.1 3.8 %all-to-all-start.2 = ((bf16[8,1,64,256]{3,2,1,0:T(8,128)(2,1)}), bf16[8,1,64,256]{3,2,1,0:T(8,128)(2,1)S(1)}, u32[]{:S(2)}, u32[]{:S(2)}) async-start(bf16[8,1,64,256]{3,2,1,0:T(8,128)(2,1)} %copy.114), calls=%async_computation.2 | async-start | bytes 524288 | tf_op jit(solution)/shard_map/all_to_all | solution.py:173
  106.9 1.7 %fusion.24 = bf16[256,128]{1,0:T(8,128)(2,1)} fusion(f32[256,128]{1,0:T(8,128)S(1)} %fusion.138, f32[256,128]{1,0:T(8,128)S(1)} %copy-done.16, bf16[256,256]{1,0:T(8,128)(2,1)S(1)} %bitcast.314, bf16[256,128]{1,0:T(8,128)(2,1)S(1)} %copy-done.5, f32[256,256]{1,0:T(8,128)S(1)} %copy-done.7, bf16[3,3,256,128]{3,2,1,0:T(8,128)(2,1)} %param.29), kind=kOutput, calls=%fused_computation.69 | convolution fusion | flops 17137664 | bytes 720896 | tf_op jit(solution)/shard_map/dot_general | solution.py:67
  108.6 6.5 %all-to-all-done.2 = bf16[8,1,64,256]{3,2,1,0:T(8,128)(2,1)S(1)} async-done(((bf16[8,1,64,256]{3,2,1,0:T(8,128)(2,1)}), bf16[8,1,64,256]{3,2,1,0:T(8,128)(2,1)S(1)}, u32[]{:S(2)}, u32[]{:S(2)}) %all-to-all-start.2) | async-done | bytes 262176 | tf_op jit(solution)/shard_map/all_to_all | solution.py:173
  115.0 1.9 %fusion.12 = bf16[1,512,256]{2,1,0:T(8,128)(2,1)} fusion(bf16[512,256]{1,0:T(8,128)(2,1)S(1)} %bitcast.280, bf16[256,256]{1,0:T(8,128)(2,1)S(1)} %copy-done.15, bf16[1,512,256]{2,1,0:T(8,128)(2,1)} %param.17), kind=kOutput, calls=%fused_computation.28 | convolution fusion | flops 67502080 | bytes 917504 | tf_op jit(solution)/shard_map/dot_general | solution.py:175
  (172 shorter events, 45.9 us)
Async XLA Ops:
  0.6 13.9 %copy-start = (bf16[256,256]{1,0:T(8,128)(2,1)S(1)}, bf16[256,256]{1,0:T(8,128)(2,1)}, u32[]{:S(2)}) copy-start(bf16[256,256]{1,0:T(8,128)(2,1)} %param.21) | copy-start | bytes 393220
  0.6 19.1 %copy-start.9 = (bf16[1,8,32,256]{3,2,1,0:T(8,128)(2,1)S(1)}, bf16[1,8,32,256]{3,2,1,0:T(8,128)(2,1)}, u32[]{:S(2)}) copy-start(bf16[1,8,32,256]{3,2,1,0:T(8,128)(2,1)} %param.15) | copy-start | bytes 393220
  0.7 19.1 %copy-start.10 = (bf16[256,256]{1,0:T(8,128)(2,1)S(1)}, bf16[256,256]{1,0:T(8,128)(2,1)}, u32[]{:S(2)}) copy-start(bf16[256,256]{1,0:T(8,128)(2,1)} %param.20) | copy-start | bytes 393220
  1.6 43.0 %collective-permute-start.8 = (bf16[1,1,64]{2,1,0:T(2,128)(2,1)S(1)}, bf16[1,1,64]{2,1,0:T(2,128)(2,1)S(1)}, u32[]{:S(2)}, u32[]{:S(2)}) collective-permute-start(bf16[1,1,64]{2,1,0:T(2,128)(2,1)S(1)} %get-tuple-element.49), channel_id=1, source_target_pairs={{0,2},{2,0},{4,6},{6,4},{8,10},{10,8},{12,14},{14,12},{1,3},{3,1},... | collective-permute-start | bytes 392 | tf_op jit(solution)/shard_map/ppermute | solution.py:136
  4.7 42.9 %collective-permute-start.9 = (bf16[1,1,64]{2,1,0:T(2,128)(2,1)S(1)}, bf16[1,1,64]{2,1,0:T(2,128)(2,1)S(1)}, u32[]{:S(2)}, u32[]{:S(2)}) collective-permute-start(bf16[1,1,64]{2,1,0:T(2,128)(2,1)S(1)} %get-tuple-element.48), channel_id=1, source_target_pairs={{0,4},{2,6},{4,0},{6,2},{8,12},{10,14},{12,8},{14,10},{1,5},{3,7},... | collective-permute-start | bytes 392 | tf_op jit(solution)/shard_map/ppermute | solution.py:136
  6.2 42.8 %collective-permute-start.10 = (bf16[1,1,64]{2,1,0:T(2,128)(2,1)S(1)}, bf16[1,1,64]{2,1,0:T(2,128)(2,1)S(1)}, u32[]{:S(2)}, u32[]{:S(2)}) collective-permute-start(bf16[1,1,64]{2,1,0:T(2,128)(2,1)S(1)} %get-tuple-element.47), channel_id=1, source_target_pairs={{0,6},{2,4},{4,2},{6,0},{8,14},{10,12},{12,10},{14,8},{1,7},{3,5},... | collective-permute-start | bytes 392 | tf_op jit(solution)/shard_map/ppermute | solution.py:136
  7.6 63.8 %all-to-all-start.1 = ((bf16[1,8,64]{2,0,1:T(2,128)(2,1)}), bf16[1,8,64]{2,0,1:T(2,128)(2,1)S(1)}, u32[]{:S(2)}, u32[]{:S(2)}) async-start(bf16[1,8,64]{2,0,1:T(2,128)(2,1)} %reshape.280), calls=%async_computation.1 | async-start | bytes 8192 | tf_op jit(solution)/shard_map/all_to_all | solution.py:139
  33.9 3.5 %collective-permute-start = (bf16[1,32,256]{2,1,0:T(8,128)(2,1)S(1)}, bf16[1,32,256]{2,1,0:T(8,128)(2,1)S(1)}, u32[]{:S(2)}, u32[]{:S(2)}) collective-permute-start(bf16[1,32,256]{2,1,0:T(8,128)(2,1)S(1)} %get-tuple-element.42), channel_id=1, source_target_pairs={{0,1},{2,3},{4,5},{6,7},{8,9},{10,11},{12,13},{14,15},{16,17},{18,... | collective-permute-start | bytes 49160 | tf_op jit(solution)/shard_map/ppermute | solution.py:30
  36.1 3.1 %collective-permute-start.1 = (bf16[1,32,256]{2,1,0:T(8,128)(2,1)S(1)}, bf16[1,32,256]{2,1,0:T(8,128)(2,1)S(1)}, u32[]{:S(2)}, u32[]{:S(2)}) collective-permute-start(bf16[1,32,256]{2,1,0:T(8,128)(2,1)S(1)} %get-tuple-element.2), channel_id=1, source_target_pairs={{1,0},{3,2},{5,4},{7,6},{9,8},{11,10},{13,12},{15,14},{17,16},{19,... | collective-permute-start | bytes 49160 | tf_op jit(solution)/shard_map/ppermute | solution.py:31
  40.9 18.4 %copy-start.2 = (bf16[3,3,256,128]{3,2,1,0:T(8,128)(2,1)S(1)}, bf16[3,3,256,128]{3,2,1,0:T(8,128)(2,1)}, u32[]{:S(2)}) copy-start(bf16[3,3,256,128]{3,2,1,0:T(8,128)(2,1)} %param.29) | copy-start | bytes 1769476
  41.2 18.0 %collective-permute-start.2 = (bf16[1,32,256]{2,1,0:T(8,128)(2,1)S(1)}, bf16[1,32,256]{2,1,0:T(8,128)(2,1)S(1)}, u32[]{:S(2)}, u32[]{:S(2)}) collective-permute-start(bf16[1,32,256]{2,1,0:T(8,128)(2,1)S(1)} %get-tuple-element.40), channel_id=1, source_target_pairs={{0,1},{2,3},{4,5},{6,7},{8,9},{10,11},{12,13},{14,15},{16,17},{18,... | collective-permute-start | bytes 49160 | tf_op jit(solution)/shard_map/ppermute | solution.py:30
  43.2 15.9 %collective-permute-start.3 = (bf16[1,32,256]{2,1,0:T(8,128)(2,1)S(1)}, bf16[1,32,256]{2,1,0:T(8,128)(2,1)S(1)}, u32[]{:S(2)}, u32[]{:S(2)}) collective-permute-start(bf16[1,32,256]{2,1,0:T(8,128)(2,1)S(1)} %get-tuple-element.41), channel_id=1, source_target_pairs={{1,0},{3,2},{5,4},{7,6},{9,8},{11,10},{13,12},{15,14},{17,16},{19,... | collective-permute-start | bytes 49160 | tf_op jit(solution)/shard_map/ppermute | solution.py:31
  44.6 7.7 %collective-permute-start.11 = (bf16[1,1,64]{2,1,0:T(2,128)(2,1)S(1)}, bf16[1,1,64]{2,1,0:T(2,128)(2,1)S(1)}, u32[]{:S(2)}, u32[]{:S(2)}) collective-permute-start(bf16[1,1,64]{2,1,0:T(2,128)(2,1)S(1)} %get-tuple-element.46), channel_id=1, source_target_pairs={{0,8},{2,10},{4,12},{6,14},{8,0},{10,2},{12,4},{14,6},{1,9},{3,11}... | collective-permute-start | bytes 392 | tf_op jit(solution)/shard_map/ppermute | solution.py:136
  47.5 6.3 %collective-permute-start.12 = (bf16[1,1,64]{2,1,0:T(2,128)(2,1)S(1)}, bf16[1,1,64]{2,1,0:T(2,128)(2,1)S(1)}, u32[]{:S(2)}, u32[]{:S(2)}) collective-permute-start(bf16[1,1,64]{2,1,0:T(2,128)(2,1)S(1)} %get-tuple-element.45), channel_id=1, source_target_pairs={{0,10},{2,8},{4,14},{6,12},{8,2},{10,0},{12,6},{14,4},{1,11},{3,9}... | collective-permute-start | bytes 392 | tf_op jit(solution)/shard_map/ppermute | solution.py:136
  49.0 5.4 %collective-permute-start.13 = (bf16[1,1,64]{2,1,0:T(2,128)(2,1)S(1)}, bf16[1,1,64]{2,1,0:T(2,128)(2,1)S(1)}, u32[]{:S(2)}, u32[]{:S(2)}) collective-permute-start(bf16[1,1,64]{2,1,0:T(2,128)(2,1)S(1)} %get-tuple-element.44), channel_id=1, source_target_pairs={{0,12},{2,14},{4,8},{6,10},{8,4},{10,6},{12,0},{14,2},{1,13},{3,15... | collective-permute-start | bytes 392 | tf_op jit(solution)/shard_map/ppermute | solution.py:136
  52.3 6.3 %collective-permute-start.14 = (bf16[1,1,64]{2,1,0:T(2,128)(2,1)S(1)}, bf16[1,1,64]{2,1,0:T(2,128)(2,1)S(1)}, u32[]{:S(2)}, u32[]{:S(2)}) collective-permute-start(bf16[1,1,64]{2,1,0:T(2,128)(2,1)S(1)} %get-tuple-element.43), channel_id=1, source_target_pairs={{0,14},{2,12},{4,10},{6,8},{8,6},{10,4},{12,2},{14,0},{1,15},{3,13... | collective-permute-start | bytes 392 | tf_op jit(solution)/shard_map/ppermute | solution.py:136
  61.0 2.6 %collective-permute-start.4 = (bf16[1,32,256]{2,1,0:T(8,128)(2,1)S(1)}, bf16[1,32,256]{2,1,0:T(8,128)(2,1)S(1)}, u32[]{:S(2)}, u32[]{:S(2)}) collective-permute-start(bf16[1,32,256]{2,1,0:T(8,128)(2,1)S(1)} %get-tuple-element.38), channel_id=1, source_target_pairs={{0,1},{2,3},{4,5},{6,7},{8,9},{10,11},{12,13},{14,15},{16,17},{18,... | collective-permute-start | bytes 49160 | tf_op jit(solution)/shard_map/ppermute | solution.py:30
  62.3 3.1 %collective-permute-start.5 = (bf16[1,32,256]{2,1,0:T(8,128)(2,1)S(1)}, bf16[1,32,256]{2,1,0:T(8,128)(2,1)S(1)}, u32[]{:S(2)}, u32[]{:S(2)}) collective-permute-start(bf16[1,32,256]{2,1,0:T(8,128)(2,1)S(1)} %get-tuple-element.39), channel_id=1, source_target_pairs={{1,0},{3,2},{5,4},{7,6},{9,8},{11,10},{13,12},{15,14},{17,16},{19,... | collective-permute-start | bytes 49160 | tf_op jit(solution)/shard_map/ppermute | solution.py:31
  68.0 7.0 %collective-permute-start.6 = (bf16[1,32,256]{2,1,0:T(8,128)(2,1)S(1)}, bf16[1,32,256]{2,1,0:T(8,128)(2,1)S(1)}, u32[]{:S(2)}, u32[]{:S(2)}) collective-permute-start(bf16[1,32,256]{2,1,0:T(8,128)(2,1)S(1)} %get-tuple-element.36), channel_id=1, source_target_pairs={{0,1},{2,3},{4,5},{6,7},{8,9},{10,11},{12,13},{14,15},{16,17},{18,... | collective-permute-start | bytes 49160 | tf_op jit(solution)/shard_map/ppermute | solution.py:30
  70.1 4.9 %collective-permute-start.7 = (bf16[1,32,256]{2,1,0:T(8,128)(2,1)S(1)}, bf16[1,32,256]{2,1,0:T(8,128)(2,1)S(1)}, u32[]{:S(2)}, u32[]{:S(2)}) collective-permute-start(bf16[1,32,256]{2,1,0:T(8,128)(2,1)S(1)} %get-tuple-element.37), channel_id=1, source_target_pairs={{1,0},{3,2},{5,4},{7,6},{9,8},{11,10},{13,12},{15,14},{17,16},{19,... | collective-permute-start | bytes 49160 | tf_op jit(solution)/shard_map/ppermute | solution.py:31
  71.4 13.5 %all-to-all-start = ((bf16[1,8,64,256]{3,2,0,1:T(8,128)(2,1)}), bf16[1,8,64,256]{3,2,0,1:T(8,128)(2,1)S(1)}, u32[]{:S(2)}, u32[]{:S(2)}) async-start(bf16[1,8,64,256]{3,2,0,1:T(8,128)(2,1)} %bitcast.61), calls=%async_computation | async-start | bytes 524288 | tf_op jit(solution)/shard_map/all_to_all | solution.py:124
  76.9 8.0 %copy-start.12 = (bf16[256,256]{1,0:T(8,128)(2,1)S(1)}, bf16[256,256]{1,0:T(8,128)(2,1)}, u32[]{:S(2)}) copy-start(bf16[256,256]{1,0:T(8,128)(2,1)} %param.24) | copy-start | bytes 393220
  101.2 13.9 %copy-start.15 = (bf16[256,256]{1,0:T(8,128)(2,1)S(1)}, bf16[256,256]{1,0:T(8,128)(2,1)}, u32[]{:S(2)}) copy-start(bf16[256,256]{1,0:T(8,128)(2,1)} %param.27) | copy-start | bytes 393220
  102.1 13.0 %all-to-all-start.2 = ((bf16[8,1,64,256]{3,2,1,0:T(8,128)(2,1)}), bf16[8,1,64,256]{3,2,1,0:T(8,128)(2,1)S(1)}, u32[]{:S(2)}, u32[]{:S(2)}) async-start(bf16[8,1,64,256]{3,2,1,0:T(8,128)(2,1)} %copy.114), calls=%async_computation.2 | async-start | bytes 524288 | tf_op jit(solution)/shard_map/all_to_all | solution.py:173
  (13 other events, 49.1 us)
